TPU v7x, 1024 devices: a whole 4x4x32 slice. The times are simulated.
1024 devices in a mesh: dp: 4 (over x), ctx: 32 (over z), tp: 8 (over y, core).
Axes of the slice: x: 4, y: 4, z: 32, core: 2. Of those that a mesh axis runs over, the one named last changes fastest.
Arguments:
- queries: bfloat16 [16384, 4096], P(('dp', 'ctx'), 'tp'), parts along dimension 0, may hold values from -25 to 25
- keys: bfloat16 [16384, 1024], P(('dp', 'ctx'), 'tp'), parts along dimension 0, may hold values from -6 to 6
- values: bfloat16 [16384, 1024], P(('dp', 'ctx'), 'tp'), parts along dimension 0, may hold values from -6 to 6
- counts: int32 [128, 32], P('dp'), parts along dimension 0, may hold values from 0 to 8, as said below
- doc_lengths: int32 [64], P('dp'), parts along dimension 0, may hold values from 1 to 2048, 4096 in all
Outputs:
- attended: bfloat16 [16384, 4096], P(('dp', 'ctx'), 'tp'), parts along dimension 0
There are 4 independent parts, one for each index of `dp`. A program takes and returns all parts, laid end to end along the dimension named above; each array names one. Nothing has to cross between parts.
Inputs may be any that keep to these rules, and one draw needn't show every extreme that they name: Every row and every column of counts sums to 128; no entry exceeds 8, and some entry equals 8.
All inputs are finite; a program needn't handle non-finite values.
Results may differ from a plain program's by a relative error of at most 0.006.
Values may be sent and summed in bfloat16 or wider, within the bound.
No kernel may reach another device: no remote copies, remote signals or barrier semaphores. Data moves between devices by JAX's collectives and lax.ppermute only.
A program may use at most 32 MiB of HBM per device.

v0:
```python
import jax
import jax.numpy as jnp
from jax import lax
from jax.sharding import PartitionSpec as P

HQ = 32
KVH = 8
HD = 128


def span_pos(owner, local, half, ncx):
    return jnp.where(
        local < half, owner * half + local, (2 * ncx - 1 - owner) * half + local - half
    )


def segment_of(places, doc_ends):
    return jnp.sum((doc_ends[None, :] <= places[:, None]).astype(jnp.int32), axis=1)


def make_fold(query_own, query_pos, query_seg, key_pos_all, doc_ends, kv_local, group):
    tok = query_own.shape[0]
    query_four = query_own.reshape(tok, kv_local, group, HD)
    scale = 1.0 / HD**0.5

    def attend(carry, key_rows, value_rows, key_pos):
        visible = (key_pos[None, :] <= query_pos[:, None]) & (
            segment_of(key_pos, doc_ends)[None, :] == query_seg[:, None]
        )
        count = key_rows.shape[0]
        key_three = key_rows.reshape(count, kv_local, HD)
        value_three = value_rows.reshape(count, kv_local, HD)
        top_old, total_old, accum_old = carry
        scores = (
            jnp.einsum("qcgd,kcd->cgqk", query_four, key_three, preferred_element_type=jnp.float32)
            * scale
        )
        masked = jnp.where(visible, scores, -1e30)
        top_new = jnp.maximum(top_old, jnp.max(masked, axis=-1))
        factor = jnp.exp(top_old - top_new)
        expo = jnp.where(visible, jnp.exp(masked - top_new[..., None]), 0.0)
        total_new = total_old * factor + jnp.sum(expo, axis=-1)
        weights = expo.astype(jnp.bfloat16)
        accum_new = accum_old * factor[..., None] + jnp.einsum(
            "cgqk,kcd->cgqd", weights, value_three, preferred_element_type=jnp.float32
        )
        return (top_new, total_new, accum_new)

    def fold(carry, piece, start):
        key_rows, value_rows = piece
        count = key_rows.shape[0]
        width = 512
        blocks = count // width

        def step(state, item):
            return (attend(state, item[0], item[1], item[2]), None)

        stacked = (
            key_rows.reshape(blocks, width, key_rows.shape[1]),
            value_rows.reshape(blocks, width, value_rows.shape[1]),
            key_pos_all.reshape(blocks, width),
        )
        result, _ = lax.scan(step, carry, stacked)
        return result

    return fold


def body(queries, keys, values, counts, doc_lengths):
    ncx = lax.axis_size("ctx")
    me = lax.axis_index("ctx")
    tok = queries.shape[0]
    half = tok // 2
    slot = 2 * tok // ncx
    kv_local = keys.shape[1] // HD
    group = HQ // KVH
    ends = jnp.cumsum(counts, axis=1)
    starts = ends - counts
    column_end = jnp.cumsum(counts, axis=0)
    column_pre = column_end - counts
    my_start = jnp.take(starts, me, axis=0)
    my_count = jnp.take(counts, me, axis=0)
    offsets = jnp.arange(slot, dtype=jnp.int32)
    send_index = (my_start[:, None] + offsets[None, :]).reshape(-1)
    send_valid = (offsets[None, :] < my_count[:, None]).reshape(-1)
    send_index = jnp.clip(send_index, 0, tok - 1)

    def pack(rows):
        picked = jnp.take(rows, send_index, axis=0)
        return jnp.where(send_valid[:, None], picked, jnp.zeros_like(picked))

    local_ids = jnp.arange(tok, dtype=jnp.int32)
    pre_here = jnp.take(column_pre, me, axis=1)
    end_here = jnp.take(column_end, me, axis=1)
    source = jnp.sum((end_here[None, :] <= local_ids[:, None]).astype(jnp.int32), axis=1)
    recv_index = source * slot + local_ids - jnp.take(pre_here, source)

    def unpack(rows):
        return jnp.take(rows, recv_index, axis=0)

    doc_ends = jnp.cumsum(doc_lengths)
    query_pos = span_pos(me + 0 * local_ids, local_ids, half, ncx)
    query_seg = segment_of(query_pos, doc_ends)
    rows_all_ids = jnp.arange(ncx * tok, dtype=jnp.int32)
    state = (
        jnp.full((kv_local, group, tok), -1e30, jnp.float32),
        jnp.zeros((kv_local, group, tok), jnp.float32),
        jnp.zeros((kv_local, group, tok, HD), jnp.float32),
    )
    got_q, got_k, got_v = (
        lax.all_to_all(pack(queries), "ctx", split_axis=0, concat_axis=0, tiled=True),
        lax.all_to_all(pack(keys), "ctx", split_axis=0, concat_axis=0, tiled=True),
        lax.all_to_all(pack(values), "ctx", split_axis=0, concat_axis=0, tiled=True),
    )
    query_own = unpack(got_q)
    key_pos_all = span_pos(rows_all_ids // tok, rows_all_ids % tok, half, ncx)
    fold = make_fold(query_own, query_pos, query_seg, key_pos_all, doc_ends, kv_local, group)
    result = fold(
        state,
        (
            lax.all_gather(unpack(got_k), "ctx", axis=0, tiled=True),
            lax.all_gather(unpack(got_v), "ctx", axis=0, tiled=True),
        ),
        jnp.int32(0),
    )
    top_final, total_final, accum_final = result
    mixed = accum_final / total_final[..., None]
    return (
        jnp.transpose(mixed, (2, 0, 1, 3)).reshape(tok, kv_local * group * HD).astype(jnp.bfloat16)
    )


def solution(mesh):
    placed = (
        P(("dp", "ctx"), "tp"),
        P(("dp", "ctx"), "tp"),
        P(("dp", "ctx"), "tp"),
        P("dp", None),
        P("dp"),
    )
    return jax.shard_map(
        body, mesh=mesh, in_specs=placed, out_specs=P(("dp", "ctx"), "tp"), check_vma=False
    )
```

profile of v0, /device:TPU:6, one launch (start us, length us, event | category | flops | bytes accessed | tf_op | source)
XLA Modules:
  0.0 380.0 jit_solution(13069162221682149827)
XLA Ops:
  8.2 0.9 gather_fusion.3
  9.1 0.9 gather_fusion.5
  10.0 0.8 fusion.23
  10.7 28.7 %all-to-all-start = ((bf16[32,8,128]{2,1,0:T(8,128)(2,1)}), bf16[32,8,128]{2,1,0:T(8,128)(2,1)S(1)}, u32[]{:S(2)}, u32[]{:S(2)}) async-start(bf16[32,8,128]{2,1,0:T(8,128)(2,1)} %get-tuple-element.169), calls=%async_computation | async-start | bytes 131072 | tf_op jit(solution)/shard_map/all_to_all | solution.py:112
  39.8 25.4 %all-to-all-done = bf16[32,8,128]{2,1,0:T(8,128)(2,1)S(1)} async-done(((bf16[32,8,128]{2,1,0:T(8,128)(2,1)}), bf16[32,8,128]{2,1,0:T(8,128)(2,1)S(1)}, u32[]{:S(2)}, u32[]{:S(2)}) %all-to-all-start) | async-done | bytes 65568 | tf_op jit(solution)/shard_map/all_to_all | solution.py:112
  65.3 3.9 %all-to-all-start.2 = ((bf16[32,8,128]{2,1,0:T(8,128)(2,1)}), bf16[32,8,128]{2,1,0:T(8,128)(2,1)S(1)}, u32[]{:S(2)}, u32[]{:S(2)}) async-start(bf16[32,8,128]{2,1,0:T(8,128)(2,1)} %get-tuple-element.168), calls=%async_computation.2 | async-start | bytes 131072 | tf_op jit(solution)/shard_map/all_to_all | solution.py:113
  69.2 1.2 gather_fusion
  71.2 22.5 %all-to-all-done.2 = bf16[32,8,128]{2,1,0:T(8,128)(2,1)S(1)} async-done(((bf16[32,8,128]{2,1,0:T(8,128)(2,1)}), bf16[32,8,128]{2,1,0:T(8,128)(2,1)S(1)}, u32[]{:S(2)}, u32[]{:S(2)}) %all-to-all-start.2) | async-done | bytes 65568 | tf_op jit(solution)/shard_map/all_to_all | solution.py:113
  95.2 1.2 gather_fusion.1
  96.3 0.9 fusion.21
  97.2 3.9 %all-to-all-start.1 = ((bf16[32,8,512]{2,1,0:T(8,128)(2,1)}), bf16[32,8,512]{2,1,0:T(8,128)(2,1)S(1)}, u32[]{:S(2)}, u32[]{:S(2)}) async-start(bf16[32,8,512]{2,1,0:T(8,128)(2,1)} %fusion.21), calls=%async_computation.1 | async-start | bytes 524288 | tf_op jit(solution)/shard_map/all_to_all | solution.py:111
  102.9 39.8 %all-to-all-done.1 = bf16[32,8,512]{2,1,0:T(8,128)(2,1)S(1)} async-done(((bf16[32,8,512]{2,1,0:T(8,128)(2,1)}), bf16[32,8,512]{2,1,0:T(8,128)(2,1)S(1)}, u32[]{:S(2)}, u32[]{:S(2)}) %all-to-all-start.1) | async-done | bytes 262176 | tf_op jit(solution)/shard_map/all_to_all | solution.py:111
  142.8 0.8 gather_fusion.2
  143.8 72.3 %all-gather.5.cloned.1.call-done = bf16[4096,128]{1,0:T(8,128)(2,1)} async-done(((bf16[128,128]{1,0:T(8,128)(2,1)}), bf16[4096,128]{1,0:T(8,128)(2,1)}) %all-gather.5.cloned.1.call-update) | async-done | bytes 1048592 | tf_op jit(solution)/shard_map/all_gather | solution.py:122
  216.1 130.9 %all-gather.3.cloned.1.call-done = bf16[4096,128]{1,0:T(8,128)(2,1)} async-done(((bf16[128,128]{1,0:T(8,128)(2,1)}), bf16[4096,128]{1,0:T(8,128)(2,1)}) %all-gather.3.cloned.1.call-update) | async-done | bytes 1048592 | tf_op jit(solution)/shard_map/all_gather | solution.py:121
  346.9 25.3 %while.17 = (s32[]{:T(128)}, f32[1,4,128]{2,1,0:T(4,128)S(1)}, f32[1,4,128]{2,1,0:T(4,128)S(1)}, f32[1,4,128,128]{3,2,1,0:T(8,128)S(1)}, s32[8,512]{1,0:T(8,128)...) while((s32[]{:T(128)}, f32[1,4,128]{2,1,0:T(4,128)S(1)}, ...), condition=%wide.region_9.14_spmd.clone, body=%wide.region_5.13_spmd.clone.sunk | while | flops 136998016 | bytes 4373213 | solution.py:63
  347.2 1.2 fusion.47
  348.5 1.3 fusion.50
  350.4 1.2 fusion.47
  351.7 1.3 fusion.50
  353.6 1.2 fusion.47
  354.8 1.3 fusion.50
  356.7 1.2 fusion.47
  358.0 1.3 fusion.50
  359.9 1.2 fusion.47
  361.1 1.3 fusion.50
  363.1 1.2 fusion.47
  364.3 1.3 fusion.50
  366.2 1.2 fusion.47
  367.5 1.3 fusion.50
  369.4 1.2 fusion.47
  370.6 1.3 fusion.50
  (116 shorter events, 11.4 us)
Async XLA Ops:
  6.5 88.7 %copy-start = (bf16[128,512]{1,0:T(8,128)(2,1)S(1)}, bf16[128,512]{1,0:T(8,128)(2,1)}, u32[]{:S(2)}) copy-start(bf16[128,512]{1,0:T(8,128)(2,1)} %param.15) | copy-start | bytes 393220
  6.5 0.8 copy-start.3
  7.5 0.8 copy-start.1
  8.2 0.9 copy-start.2
  10.7 54.5 %all-to-all-start = ((bf16[32,8,128]{2,1,0:T(8,128)(2,1)}), bf16[32,8,128]{2,1,0:T(8,128)(2,1)S(1)}, u32[]{:S(2)}, u32[]{:S(2)}) async-start(bf16[32,8,128]{2,1,0:T(8,128)(2,1)} %get-tuple-element.169), calls=%async_computation | async-start | bytes 131072 | tf_op jit(solution)/shard_map/all_to_all | solution.py:112
  65.3 28.4 %all-to-all-start.2 = ((bf16[32,8,128]{2,1,0:T(8,128)(2,1)}), bf16[32,8,128]{2,1,0:T(8,128)(2,1)S(1)}, u32[]{:S(2)}, u32[]{:S(2)}) async-start(bf16[32,8,128]{2,1,0:T(8,128)(2,1)} %get-tuple-element.168), calls=%async_computation.2 | async-start | bytes 131072 | tf_op jit(solution)/shard_map/all_to_all | solution.py:113
  69.1 146.9 %all-gather.5.cloned.1.call-start = ((), (), s32[]{:S(2)}) async-start(), calls=%async_computation.4 | async-start | bytes 1081344 | tf_op jit(solution)/shard_map/all_gather | solution.py:122
  97.2 45.6 %all-to-all-start.1 = ((bf16[32,8,512]{2,1,0:T(8,128)(2,1)}), bf16[32,8,512]{2,1,0:T(8,128)(2,1)S(1)}, u32[]{:S(2)}, u32[]{:S(2)}) async-start(bf16[32,8,512]{2,1,0:T(8,128)(2,1)} %fusion.21), calls=%async_computation.1 | async-start | bytes 524288 | tf_op jit(solution)/shard_map/all_to_all | solution.py:111
  101.1 245.8 %all-gather.3.cloned.1.call-start = ((), (), s32[]{:S(2)}) async-start(), calls=%async_computation.3 | async-start | bytes 1081344 | tf_op jit(solution)/shard_map/all_gather | solution.py:121
  101.9 0.7 copy-start.4
Sparse Core Ops, SparseCore 0:
  95.2 120.8 all-gather.4
  218.7 128.1 all-gather.2
where the time goes:
time: 381 us; the launch traced here: 380 us
  waiting for transfers between devices  292 us (77%)
  starting transfers between devices  36.5 us (10%)
  matrix products  20.5 us (5%)
  between operations  13.6 us (4%)
  local copies, waits for them, and re-layouts  9.37 us (2%)
  other arithmetic  7.83 us (2%)
    all_gather x1, waiting for transfers between devices, body(): lax.all_gather(unpack(got_k), 'ctx', axis=0, tiled=True)  131 us
    all_gather x1, waiting for transfers between devices, body(): lax.all_gather(unpack(got_v), 'ctx', axis=0, tiled=True)  72.3 us
    all_to_all x1, waiting for transfers between devices, body(): lax.all_to_all(pack(queries), 'ctx', split_axis=0, concat_axis=0, tiled=T...  39.8 us
    all_to_all x1, starting transfers between devices, body(): lax.all_to_all(pack(keys), 'ctx', split_axis=0, concat_axis=0, tiled=True)  28.7 us
    all_to_all x1, waiting for transfers between devices, body(): lax.all_to_all(pack(keys), 'ctx', split_axis=0, concat_axis=0, tiled=True)  25.4 us
    all_to_all x1, waiting for transfers between devices, body(): lax.all_to_all(pack(values), 'ctx', split_axis=0, concat_axis=0, tiled=True)  22.5 us
    dot_general x8, matrix products, attend(): jnp.einsum('cgqk,kcd->cgqd', weights, value_three, preferred_element_type...  10.8 us
    dot_general x8, matrix products, attend(): jnp.einsum('qcgd,kcd->cgqk', query_four, key_three, preferred_element_typ...  9.73 us
  transfers between devices with their start and end apart: 5, of which 5 were waited for; matrix products, arithmetic and copies ran while one was open for 2% of the time, Pallas kernels for 0%

commit v1 on v0

v1 whole, which is shorter than its diff:
```python
import jax
import jax.numpy as jnp
from jax import lax
from jax.experimental import pallas as pl
from jax.experimental.pallas import tpu as pltpu
from jax.sharding import PartitionSpec as P

HQ = 32
KVH = 8
HD = 128
GROUP = HQ // KVH
TOK = 128
HALF = 64
NCX = 32
SLOT = 8
SEQ = NCX * TOK
BLOCK = 256
LOG2E = 1.4426950408889634

f32 = jnp.float32
bf16 = jnp.bfloat16
i32 = jnp.int32


def iota(shape, dim):
    return lax.broadcasted_iota(i32, shape, dim)


def pack_kernel(counts_ref, q_ref, out_ref):
    me = lax.axis_index("ctx")
    row = counts_ref[pl.ds(me, 1), :].astype(f32)
    slots = NCX * SLOT
    owner_of = iota((slots, NCX), 0) // SLOT
    owner = iota((slots, NCX), 1)
    start = jnp.sum(jnp.where(owner < owner_of, row, 0.0), axis=1, keepdims=True)
    count = jnp.sum(jnp.where(owner == owner_of, row, 0.0), axis=1, keepdims=True)
    j = (iota((slots, 1), 0) % SLOT).astype(f32)
    want = jnp.where(j < count, start + j, -1.0)
    pick = jnp.where(iota((slots, TOK), 1).astype(f32) == want, 1.0, 0.0).astype(bf16)
    out_ref[...] = jnp.dot(pick, q_ref[...], preferred_element_type=f32).astype(bf16)


def place_kernel(counts_ref, pos_ref):
    counts = counts_ref[...].astype(f32)
    a, b = iota((NCX, NCX), 0), iota((NCX, NCX), 1)
    starts = jnp.dot(counts, (a < b).astype(f32), preferred_element_type=f32)
    before = jnp.dot((b < a).astype(f32), counts, preferred_element_type=f32)
    row = iota((NCX, TOK), 1).astype(f32)
    pos = jnp.zeros((NCX, TOK), f32)
    for o in range(NCX):
        j = row - starts[:, o : o + 1]
        local = before[:, o : o + 1] + j
        here = jnp.where(local < HALF, local + o * HALF, local + ((2 * NCX - 1 - o) * HALF - HALF))
        pos = jnp.where((j >= 0) & (j < counts[:, o : o + 1]), here, pos)
    pos_ref[...] = pos


def attend_kernel(docs_ref, counts_ref, pos_ref, q_ref, kv_ref, out_ref, s_ref, top_ref, acc_ref, sum_ref):
    me = lax.axis_index("ctx")
    slots = NCX * SLOT
    counts = counts_ref[...].astype(f32)
    mine = jnp.sum(jnp.where(iota((NCX, NCX), 1) == me, counts, 0.0), axis=1, keepdims=True)
    src_of, src = iota((NCX, slots), 1) // SLOT, iota((NCX, slots), 0)
    before = jnp.sum(jnp.where(src < src_of, mine, 0.0), axis=0, keepdims=True)
    count = jnp.sum(jnp.where(src == src_of, mine, 0.0), axis=0, keepdims=True)
    j = (iota((1, slots), 1) % SLOT).astype(f32)
    local = jnp.where(j < count, before + j, -1.0)
    pick = jnp.where(iota((TOK, slots), 0).astype(f32) == local, 1.0, 0.0).astype(bf16)
    query = jnp.dot(pick, q_ref[...], preferred_element_type=f32).astype(bf16)

    q_id = iota((TOK, HD), 0)
    q_pos = jnp.where(q_id < HALF, me * HALF + q_id, (2 * NCX - 1 - me) * HALF + q_id - HALF)
    q_first = jnp.zeros((TOK, HD), i32)
    end = jnp.int32(0)
    for d in range(docs_ref.shape[0]):
        end = end + docs_ref[d]
        q_first = jnp.where(q_pos >= end, end, q_first)
    q_pos, q_first = q_pos.astype(f32), q_first.astype(f32)

    per = BLOCK // TOK
    top_ref[...] = jnp.full(top_ref.shape, -1e30, f32)
    for blk in range(SEQ // BLOCK):
        keys = kv_ref[blk * BLOCK : (blk + 1) * BLOCK, :HD]
        seen = []
        for c in range(per):
            k_pos = pos_ref[blk * per + c : blk * per + c + 1, :]
            seen.append((k_pos <= q_pos) & (k_pos >= q_first))
        for h in range(GROUP):
            s = lax.dot_general(
                query[:, h * HD : (h + 1) * HD], keys, (((1,), (1,)), ((), ())), preferred_element_type=f32
            )
            top = top_ref[h]
            for c in range(per):
                part = jnp.where(seen[c], s[:, c * TOK : (c + 1) * TOK], -1e30)
                s_ref[h, :, blk * BLOCK + c * TOK : blk * BLOCK + (c + 1) * TOK] = part
                top = jnp.maximum(top, part)
            top_ref[h] = top
    for h in range(GROUP):
        top_ref[h] = jnp.broadcast_to(jnp.max(top_ref[h], axis=1, keepdims=True), (TOK, HD))
    c2 = LOG2E / HD**0.5
    acc_ref[...] = jnp.zeros(acc_ref.shape, f32)
    sum_ref[...] = jnp.zeros(sum_ref.shape, f32)
    for blk in range(SEQ // BLOCK):
        vals = kv_ref[blk * BLOCK : (blk + 1) * BLOCK, HD:]
        for h in range(GROUP):
            top = top_ref[h]
            total = sum_ref[h]
            weights = []
            for c in range(per):
                part = s_ref[h, :, blk * BLOCK + c * TOK : blk * BLOCK + (c + 1) * TOK]
                e = jnp.exp2((part - top) * c2)
                total = total + e
                weights.append(e.astype(bf16))
            sum_ref[h] = total
            acc_ref[h] += jnp.dot(jnp.concatenate(weights, axis=1), vals, preferred_element_type=f32)
    for h in range(GROUP):
        total = jnp.sum(sum_ref[h], axis=1, keepdims=True)
        out_ref[:, h * HD : (h + 1) * HD] = (acc_ref[h] / total).astype(bf16)


VMEM = pl.BlockSpec(memory_space=pltpu.VMEM)
SMEM = pl.BlockSpec(memory_space=pltpu.SMEM)


def body(queries, keys, values, counts, doc_lengths):
    slots = NCX * SLOT
    packed = pl.pallas_call(
        pack_kernel,
        out_shape=jax.ShapeDtypeStruct((slots, GROUP * HD), bf16),
        in_specs=[VMEM, VMEM],
        out_specs=VMEM,
        name="pack",
    )(counts, queries)
    got = lax.all_to_all(
        packed.reshape(NCX, SLOT, GROUP * HD), "ctx", split_axis=0, concat_axis=0, tiled=True
    ).reshape(slots, GROUP * HD)
    key_value = lax.all_gather(jnp.concatenate([keys, values], axis=1), "ctx", axis=0, tiled=True)
    pos = pl.pallas_call(
        place_kernel,
        out_shape=jax.ShapeDtypeStruct((NCX, TOK), f32),
        in_specs=[VMEM],
        out_specs=VMEM,
        name="place",
    )(counts)
    return pl.pallas_call(
        attend_kernel,
        out_shape=jax.ShapeDtypeStruct((TOK, GROUP * HD), bf16),
        in_specs=[SMEM, VMEM, VMEM, VMEM, VMEM],
        out_specs=VMEM,
        scratch_shapes=[
            pltpu.VMEM((GROUP, TOK, SEQ), f32),
            pltpu.VMEM((GROUP, TOK, HD), f32),
            pltpu.VMEM((GROUP, TOK, HD), f32),
            pltpu.VMEM((GROUP, TOK, HD), f32),
        ],
        name="attend",
    )(doc_lengths, counts, pos, got, key_value)


def solution(mesh):
    placed = (
        P(("dp", "ctx"), "tp"),
        P(("dp", "ctx"), "tp"),
        P(("dp", "ctx"), "tp"),
        P("dp", None),
        P("dp"),
    )
    return jax.shard_map(
        body, mesh=mesh, in_specs=placed, out_specs=P(("dp", "ctx"), "tp"), check_vma=False
    )
```

time: 381 us -> 178 us (0.47)
  waiting for transfers between devices: 292 us -> 123 us
  matrix products: 20.5 us -> 0 us
  Pallas kernels: 0 us -> 10.7 us
  local copies, waits for them, and re-layouts: 9.37 us -> 0.01 us
  starting transfers between devices: 36.5 us -> 28.7 us
  other arithmetic: 7.83 us -> 1.41 us
    all_gather x2 -> x1, waiting for transfers between devices: 203 us -> 80 us  [body(): lax.all_gather(jnp.concatenate([keys, values], axis=1), 'ctx', axis=0, ti...]
    all_to_all x3 -> x1, waiting for transfers between devices: 87.8 us -> 42.9 us  [body(): lax.all_to_all(packed.reshape(NCX, SLOT, GROUP * HD), 'ctx', split_axis=0...]
    dot_general x16 -> x0, matrix products: 20.5 us -> none  [the longest x8 10.8 us: attend(): jnp.einsum('cgqk,kcd->cgqd', weights, value_three, preferred_element_type...]
    pallas_call x0 -> x3, Pallas kernels: none -> 10.7 us  [the longest x1 6.8 us: body(): pl.pallas_call(attend_kernel, out_shape=jax.ShapeDtypeStruct((TOK, GROUP...]
    all_to_all x3 -> x1, starting transfers between devices: 36.5 us -> 28.7 us  [body(): lax.all_to_all(packed.reshape(NCX, SLOT, GROUP * HD), 'ctx', split_axis=0...]
    gather x8 -> x0, local copies, waits for them, and re-layouts: 6.39 us -> none  [the longest x3 2.86 us: pack(): picked = jnp.take(rows, send_index, axis=0)]
  transfers between devices with their start and end apart: 5 -> 2, of which waited for: 5 -> 2; matrix products, arithmetic and copies ran while one was open for 2% -> 0% of each run, Pallas kernels for 0% -> 2%
where the time goes in v1:
time: 178 us; the launch traced here: 177 us
  waiting for transfers between devices  123 us (69%)
  starting transfers between devices  28.7 us (16%)
  between operations  13.4 us (8%)
  Pallas kernels  10.7 us (6%)
    all_gather x1, waiting for transfers between devices, body(): lax.all_gather(jnp.concatenate([keys, values], axis=1), 'ctx', axis=0, ti...  80 us
    all_to_all x1, waiting for transfers between devices, body(): lax.all_to_all(packed.reshape(NCX, SLOT, GROUP * HD), 'ctx', split_axis=0...  42.9 us
    all_to_all x1, starting transfers between devices, body(): lax.all_to_all(packed.reshape(NCX, SLOT, GROUP * HD), 'ctx', split_axis=0...  28.7 us
    pallas_call x1, Pallas kernels, body(): pl.pallas_call(attend_kernel, out_shape=jax.ShapeDtypeStruct((TOK, GROUP...  6.8 us
  transfers between devices with their start and end apart: 2, of which 2 were waited for; matrix products, arithmetic and copies ran while one was open for 0% of the time, Pallas kernels for 2%

profile of v1, /device:TPU:6, one launch (start us, length us, event | category | flops | bytes accessed | tf_op | source)
XLA Modules:
  0.0 177.2 jit_solution(3198947031295325669)
XLA Ops:
  6.5 0.0 all-gather.2.cloned.1.call-start
  6.5 1.4 pad_maximum_fusion
  7.9 0.0 all-gather.2.cloned.1.call-update
  8.0 1.9 %pack.1 = bf16[256,512]{1,0:T(8,128)(2,1)} custom-call(s32[32,32]{1,0:T(8,128)} %counts_ref.5, bf16[128,512]{1,0:T(8,128)(2,1)} %q_ref.1), custom_call_target="tpu_custom_call" | custom-call | tf_op jit(solution)/shard_map/pack/pallas_call | solution.py:127
  9.9 28.7 %all-to-all-start = ((bf16[32,8,512]{2,1,0:T(8,128)(2,1)}), bf16[32,8,512]{2,1,0:T(8,128)(2,1)S(1)}, u32[]{:S(2)}, u32[]{:S(2)}) async-start(bf16[32,8,512]{2,1,0:T(8,128)(2,1)} %bitcast.2), calls=%async_computation | async-start | bytes 524288 | tf_op jit(solution)/shard_map/all_to_all | solution.py:134
  38.6 1.9 %place.1.pos_ref = f32[32,128]{1,0:T(8,128)} custom-call(s32[32,32]{1,0:T(8,128)} %counts_ref.5), custom_call_target="tpu_custom_call" | custom-call | tf_op jit(solution)/shard_map/place/pallas_call | solution.py:138
  40.6 42.9 %all-to-all-done = bf16[32,8,512]{2,1,0:T(8,128)(2,1)S(1)} async-done(((bf16[32,8,512]{2,1,0:T(8,128)(2,1)}), bf16[32,8,512]{2,1,0:T(8,128)(2,1)S(1)}, u32[]{:S(2)}, u32[]{:S(2)}) %all-to-all-start) | async-done | bytes 262176 | tf_op jit(solution)/shard_map/all_to_all | solution.py:134
  83.5 0.0 copy-start
  83.5 80.0 %all-gather.2.cloned.1.call-done.kv_ref = bf16[4096,256]{1,0:T(8,128)(2,1)} async-done(((bf16[128,256]{1,0:T(8,128)(2,1)}), bf16[4096,256]{1,0:T(8,128)(2,1)}) %all-gather.2.cloned.1.call-update) | async-done | bytes 2097168 | tf_op jit(solution)/shard_map/all_gather | solution.py:137
  163.6 0.0 copy-done
  163.6 6.8 %attend.1 = bf16[128,512]{1,0:T(8,128)(2,1)} custom-call(s32[16]{0:T(128)} %docs_ref.1, s32[32,32]{1,0:T(8,128)} %counts_ref.5, f32[32,128]{1,0:T(8,128)} %place.1.pos_ref, bf16[256,512]{1,0:T(8,128)(2,1)} %bitcast.3, bf16[4096,256]{1,0:T(8,128)(2,1)} %all-gather.2.cloned.1.call-done.kv_ref), custom_call_target="tpu_custom_call" | custom-call | tf_op jit(solution)/shard_map/attend/pallas_call | solution.py:145
Async XLA Ops:
  6.5 157.0 %all-gather.2.cloned.1.call-start = ((), (), s32[]{:S(2)}) async-start(), calls=%async_computation.1 | async-start | bytes 2162688 | tf_op jit(solution)/shard_map/all_gather | solution.py:137
  9.9 73.6 %all-to-all-start = ((bf16[32,8,512]{2,1,0:T(8,128)(2,1)}), bf16[32,8,512]{2,1,0:T(8,128)(2,1)S(1)}, u32[]{:S(2)}, u32[]{:S(2)}) async-start(bf16[32,8,512]{2,1,0:T(8,128)(2,1)} %bitcast.2), calls=%async_computation | async-start | bytes 524288 | tf_op jit(solution)/shard_map/all_to_all | solution.py:134
  83.5 80.0 %copy-start = (bf16[32,8,512]{2,1,0:T(8,128)(2,1)}, bf16[32,8,512]{2,1,0:T(8,128)(2,1)S(1)}, u32[]{:S(2)}) copy-start(bf16[32,8,512]{2,1,0:T(8,128)(2,1)S(1)} %all-to-all-done) | copy-start | bytes 786436
Sparse Core Ops, SparseCore 0:
  10.0 153.5 all-gather.1
